TPU v7x, 32 devices: a whole 2x2x4 slice. The times are simulated.
32 devices in a mesh: rep: 2 (over x), row: 16 (over z, y, core).
Axes of the slice: x: 2, y: 2, z: 4, core: 2. Of those that a mesh axis runs over, the one named last changes fastest.
Arguments:
- weight: bfloat16 [8192, 384], P('row'), may hold values from -0.0625 to 0.0625
- first_moment: bfloat16 [2, 8192, 384], P('rep', 'row'), may hold values from -0.29882812 to 0.29882812
- second_moment: bfloat16 [2, 8192, 384], P('rep', 'row'), may hold values from 2.9921532e-05 to 0.0029907227
- token_ids: int32 [2, 4, 1024], P('rep'), may hold values from 0 to 1535
- shared_inputs: bfloat16 [1024, 8192], P(None, 'row'), may hold values from -6 to 6
- private_inputs: bfloat16 [2, 512, 8192], P('rep', None, 'row'), may hold values from -6 to 6
- shared_targets: bfloat16 [1024, 384], replicated, may hold values from -6 to 6
- private_targets: bfloat16 [2, 512, 384], P('rep'), may hold values from -6 to 6
Outputs:
- merged: float32 [8192, 384], P(('row', 'rep'))
All inputs are finite; a program needn't handle non-finite values.
Results may differ from a plain program's by a relative error of at most 0.0005.
The roundings to bfloat16 on the way count: a program that leaves them out, or rounds other values in their place, can miss the bound.
Values sent between devices are 32-bit elements; how exact they have to be, the bound alone decides.
A program may use at most 64 MiB of HBM per device.

v0:
```python
import jax
import jax.numpy as jnp
from jax import lax
from jax.sharding import PartitionSpec as P

learn_rate = 0.001
beta_one = 0.9
beta_two = 0.95
adam_eps = 1e-08
weight_decay = 0.1
norm_eps = 1e-06


def from_partner(block, axis, bit):
    count = lax.axis_size(axis)
    route = []
    for low in range(count):
        high = low | 1 << bit
        if high != low and high < count:
            route += [(low, high), (high, low)]
    return lax.ppermute(block, axis, route)


def combine_pair(lower_vec, upper_vec, cross_dot, lower_norm, upper_norm):
    lower_coef = 1.0 - cross_dot / (2.0 * (lower_norm + norm_eps))
    upper_coef = 1.0 - cross_dot / (2.0 * (upper_norm + norm_eps))
    return lower_coef * lower_vec + upper_coef * upper_vec


def local_training(
    weight,
    first_moment,
    second_moment,
    token_ids,
    shared_inputs,
    private_inputs,
    shared_targets,
    private_targets,
):
    input_table = jnp.concatenate([shared_inputs, private_inputs[0]], axis=0)
    target_table = jnp.concatenate([shared_targets, private_targets[0]], axis=0).astype(jnp.float32)
    weight_start = weight.astype(jnp.float32)
    moment_one = first_moment[0].astype(jnp.float32)
    moment_two = second_moment[0].astype(jnp.float32)
    update_sum = jnp.zeros(weight_start.shape, jnp.float32)
    tokens_count = token_ids.shape[2]
    for step_index in range(token_ids.shape[1]):
        chosen = token_ids[0, step_index]
        tok_rows = jnp.take(input_table, chosen, axis=0)
        targets = jnp.take(target_table, chosen, axis=0)
        weight_now = weight_start - learn_rate * update_sum
        weight_bf = weight_now.astype(jnp.bfloat16)
        partial_value = jnp.dot(tok_rows, weight_bf, preferred_element_type=jnp.float32)
        output = lax.psum(partial_value, "row")
        residual = (output - targets).astype(jnp.bfloat16)
        gradient = (
            lax.dot_general(
                tok_rows, residual, (((0,), (0,)), ((), ())), preferred_element_type=jnp.float32
            )
            / tokens_count
        )
        moment_one = beta_one * moment_one + (1.0 - beta_one) * gradient
        moment_two = beta_two * moment_two + (1.0 - beta_two) * gradient * gradient
        direction = moment_one / (jnp.sqrt(moment_two) + adam_eps) + weight_decay * weight_now
        update_sum = update_sum + direction
    return update_sum


def on_device(
    weight,
    first_moment,
    second_moment,
    token_ids,
    shared_inputs,
    private_inputs,
    shared_targets,
    private_targets,
):
    update_sum = local_training(
        weight,
        first_moment,
        second_moment,
        token_ids,
        shared_inputs,
        private_inputs,
        shared_targets,
        private_targets,
    )
    replica_count = lax.axis_size("rep")
    level_count = replica_count.bit_length() - 1
    replica = lax.axis_index("rep")
    local_rows, columns = update_sum.shape
    block_rows = local_rows // replica_count
    current = update_sum
    for tree_level in range(level_count):
        own_bit = replica // 2**tree_level % 2
        received = from_partner(current, "rep", tree_level)
        lower_vec = jnp.where(own_bit == 0, current, received)
        upper_vec = jnp.where(own_bit == 0, received, current)
        local_dots = (
            jnp.sum(lower_vec * upper_vec),
            jnp.sum(lower_vec * lower_vec),
            jnp.sum(upper_vec * upper_vec),
        )
        cross_dot, lower_norm, upper_norm = lax.psum(
            (local_dots[0], local_dots[1], local_dots[2]), "row"
        )
        current = combine_pair(lower_vec, upper_vec, cross_dot, lower_norm, upper_norm)
    return lax.dynamic_slice_in_dim(current, replica * block_rows, block_rows, 0)


def solution(mesh):
    placed = (
        P("row", None),
        P("rep", "row", None),
        P("rep", "row", None),
        P("rep", None, None),
        P(None, "row"),
        P("rep", None, "row"),
        P(),
        P("rep", None, None),
    )
    return jax.shard_map(
        on_device, mesh=mesh, in_specs=placed, out_specs=P(("row", "rep"), None), check_vma=False
    )
```

profile of v0, /device:TPU:0, one launch (start us, length us, event | category | flops | bytes accessed | tf_op | source)
XLA Modules:
  0.0 485.6 jit_solution(10246385337719952556)
XLA Ops:
  6.5 0.9 fusion.64
  7.5 1.5 pad_maximum_fusion
  9.0 4.0 gather_fusion
  13.0 1.9 fusion.26
  15.0 1.4 maximum_convert_fusion
  16.4 4.8 gather_fusion.1
  21.2 6.7 %gather_fusion.2 = bf16[1024,512]{1,0:T(8,128)(2,1)} fusion(bf16[1536,512]{1,0:T(8,128)(2,1)} %copy-done, s32[1024]{0:T(1024)S(1)} %fusion.38), kind=kCustom, calls=%fused_computation.2.clone | custom fusion | bytes 2101248 | tf_op jit(solution)/shard_map/jit(_take)/gather | solution.py:49
  27.9 85.7 %all-reduce.6.cloned.1.call-done = f32[1024,384]{1,0:T(8,128)} async-done(((f32[1024,384]{1,0:T(8,128)}), f32[1024,384]{1,0:T(8,128)}) %all-reduce.6.cloned.1.call-update) | async-done | bytes 1572880 | tf_op jit(solution)/shard_map/psum | solution.py:54
  113.6 3.1 fusion.5
  116.6 0.9 copy-done.4
  117.5 2.5 fusion.27
  120.1 4.8 gather_fusion.3
  124.9 5.6 %gather_fusion.4 = bf16[1024,512]{1,0:T(8,128)(2,1)S(1)} fusion(bf16[1536,512]{1,0:T(8,128)(2,1)} %copy-done, s32[1024]{0:T(1024)S(1)} %fusion.39), kind=kCustom, calls=%fused_computation.3.clone | custom fusion | bytes 2101248 | tf_op jit(solution)/shard_map/jit(_take)/gather | solution.py:49
  130.6 84.3 %all-reduce.8.cloned.1.call-done = f32[1024,384]{1,0:T(8,128)} async-done(((f32[1024,384]{1,0:T(8,128)}), f32[1024,384]{1,0:T(8,128)}) %all-reduce.8.cloned.1.call-update) | async-done | bytes 1572880 | tf_op jit(solution)/shard_map/psum | solution.py:54
  214.9 4.0 multiply_add_fusion.2
  219.0 0.9 copy-done.18
  219.8 0.3 copy-done.20
  220.2 2.9 fusion.28
  223.3 4.8 gather_fusion.5
  228.1 6.7 %gather_fusion.6 = bf16[1024,512]{1,0:T(8,128)(2,1)} fusion(bf16[1536,512]{1,0:T(8,128)(2,1)} %copy-done, s32[1024]{0:T(1024)S(1)} %fusion.40), kind=kCustom, calls=%fused_computation.4.clone | custom fusion | bytes 2101248 | tf_op jit(solution)/shard_map/jit(_take)/gather | solution.py:49
  234.8 83.1 %all-reduce.10.cloned.1.call-done = f32[1024,384]{1,0:T(8,128)} async-done(((f32[1024,384]{1,0:T(8,128)}), f32[1024,384]{1,0:T(8,128)}) %all-reduce.10.cloned.1.call-update) | async-done | bytes 1572880 | tf_op jit(solution)/shard_map/psum | solution.py:54
  317.9 3.1 fusion.9
  321.0 0.9 copy-done.7
  322.0 3.5 fusion.29
  325.5 4.8 gather_fusion.7
  330.2 90.0 %all-reduce.12.cloned.1.call-done = f32[1024,384]{1,0:T(8,128)} async-done(((f32[1024,384]{1,0:T(8,128)}), f32[1024,384]{1,0:T(8,128)}) %all-reduce.12.cloned.1.call-update) | async-done | bytes 1572880 | tf_op jit(solution)/shard_map/psum | solution.py:54
  420.2 6.1 %add_add_fusion = f32[512,384]{1,0:T(8,128)S(1)} fusion(f32[1024,384]{1,0:T(8,128)} %all-reduce.12.cloned.1.call-done, f32[1024,384]{1,0:T(8,128)} %gather_fusion.7, bf16[512,384]{1,0:T(8,128)(2,1)} %param.12, pred[1024]{0:T(1024)(128)(4,1)S(1)} %compare_and_fusion, bf16[1024,512]{1,0:T(8,128)(2,1)S(1)} %copy-done.3, f32[512,384]{1,0:T(8,128)} %copy-done.7, ...), kind=kOutput, calls=%fused_computation.40 | convolution fusion | flops 414580736 | bytes 9307136 | tf_op jit(solution)/shard_map/dot_general | solution.py:57
  426.3 1.5 collective-permute-start
  427.8 16.8 %collective-permute-done = f32[512,384]{1,0:T(8,128)S(1)} collective-permute-done((f32[512,384]{1,0:T(8,128)S(1)}, f32[512,384]{1,0:T(8,128)S(1)}, u32[]{:S(2)}, u32[]{:S(2)}) %collective-permute-start) | collective-permute-done | bytes 786464 | tf_op jit(solution)/shard_map/ppermute | solution.py:21
  444.6 1.1 multiply_reduce_fusion.1
  445.7 30.2 %all-reduce = (f32[]{:T(128)}, f32[]{:T(128)}, f32[]{:T(128)}) all-reduce(f32[]{:T(128)} %get-tuple-element.8, f32[]{:T(128)} %get-tuple-element.9, f32[]{:T(128)} %get-tuple-element.6), channel_id=1, replica_groups=mesh['rep'=2,'row'=16] {'row'}, use_global_device_ids=true, to_apply=%region_5.8 | all-reduce | flops 3 | bytes 24 | tf_op jit(solution)/shard_map/psum | solution.py:105
  478.3 0.8 fusion.33
  (56 shorter events, 0.5 us)
Async XLA Ops:
  6.5 107.0 %all-reduce.6.cloned.1.call-start = ((), (), s32[]{:S(2)}) async-start(), calls=%async_computation | async-start | bytes 3145728 | tf_op jit(solution)/shard_map/psum | solution.py:54
  8.9 4.0 copy-start
  9.0 4.0 copy-start.8
  14.9 200.0 %all-reduce.8.cloned.1.call-start = ((), (), s32[]{:S(2)}) async-start(), calls=%async_computation.1 | async-start | bytes 3145728 | tf_op jit(solution)/shard_map/psum | solution.py:54
  113.5 4.0 copy-start.1
  113.5 4.0 copy-start.9
  113.5 4.0 copy-start.12
  113.5 4.0 copy-start.15
  116.6 0.9 copy-start.4
  120.1 197.8 %all-reduce.10.cloned.1.call-start = ((), (), s32[]{:S(2)}) async-start(), calls=%async_computation.2 | async-start | bytes 3145728 | tf_op jit(solution)/shard_map/psum | solution.py:54
  214.9 5.3 %copy-start.5 = (f32[512,384]{1,0:T(8,128)S(1)}, f32[512,384]{1,0:T(8,128)}, u32[]{:S(2)}) copy-start(f32[512,384]{1,0:T(8,128)} %copy-done.4) | copy-start | bytes 2359300
  214.9 5.3 %copy-start.10 = (bf16[512,384]{1,0:T(8,128)(2,1)S(1)}, bf16[512,384]{1,0:T(8,128)(2,1)}, u32[]{:S(2)}) copy-start(bf16[512,384]{1,0:T(8,128)(2,1)} %param.12) | copy-start | bytes 1179652
  214.9 5.3 %copy-start.13 = (bf16[1,512,384]{2,1,0:T(8,128)(2,1)S(1)}, bf16[1,512,384]{2,1,0:T(8,128)(2,1)}, u32[]{:S(2)}) copy-start(bf16[1,512,384]{2,1,0:T(8,128)(2,1)} %param.13) | copy-start | bytes 1179652
  214.9 5.3 %copy-start.16 = (bf16[1,512,384]{2,1,0:T(8,128)(2,1)S(1)}, bf16[1,512,384]{2,1,0:T(8,128)(2,1)}, u32[]{:S(2)}) copy-start(bf16[1,512,384]{2,1,0:T(8,128)(2,1)} %param.14) | copy-start | bytes 1179652
  218.9 0.9 copy-start.18
  218.9 1.2 copy-start.20
  223.1 197.1 %all-reduce.12.cloned.1.call-start = ((), (), s32[]{:S(2)}) async-start(), calls=%async_computation.3 | async-start | bytes 3145728 | tf_op jit(solution)/shard_map/psum | solution.py:54
  317.9 4.0 copy-start.2
  317.9 4.0 copy-start.6
  317.9 4.0 copy-start.11
  317.9 4.0 copy-start.14
  317.9 4.0 copy-start.17
  317.9 4.0 copy-start.19
  317.9 4.0 copy-start.21
  321.0 0.9 copy-start.7
  325.5 94.8 %copy-start.3 = (bf16[1024,512]{1,0:T(8,128)(2,1)S(1)}, bf16[1024,512]{1,0:T(8,128)(2,1)}, u32[]{:S(2)}) copy-start(bf16[1024,512]{1,0:T(8,128)(2,1)} %gather_fusion.6) | copy-start | bytes 3145732
  426.3 18.3 %collective-permute-start = (f32[512,384]{1,0:T(8,128)S(1)}, f32[512,384]{1,0:T(8,128)S(1)}, u32[]{:S(2)}, u32[]{:S(2)}) collective-permute-start(f32[512,384]{1,0:T(8,128)S(1)} %add_add_fusion), channel_id=1, source_target_pairs={{0,16},{16,0},{1,17},{17,1},{2,18},{18,2},{3,19},{19,3},{4,20},{20... | collective-permute-start | bytes 2359304 | tf_op jit(solution)/shard_map/ppermute | solution.py:21
Sparse Core Ops, SparseCore 0:
  15.0 98.4 all-reduce.5
  120.2 94.6 all-reduce.7
  223.2 94.6 all-reduce.9
  325.6 94.5 all-reduce.11
where the time goes:
time: 486 us
  waiting for transfers between devices  360 us (74%)
  local copies, waits for them, and re-layouts  46.1 us (9%)
  blocking collectives  30.2 us (6%)
  matrix products  27.1 us (6%)
  between operations  15.8 us (3%)
    psum x4, waiting for transfers between devices, local_training(): output = lax.psum(partial_value, 'row')  343 us
    psum x1, blocking collectives, on_device(): lax.psum((local_dots[0], local_dots[1], local_dots[2]), 'row')  30.2 us
    gather x4, local copies, waits for them, and re-layouts, local_training(): tok_rows = jnp.take(input_table, chosen, axis=0)  23 us
    gather x4, local copies, waits for them, and re-layouts, local_training(): targets = jnp.take(target_table, chosen, axis=0)  19.2 us
    ppermute x1, waiting for transfers between devices, from_partner(): return lax.ppermute(block, axis, route)  16.8 us
    dot_general x4, matrix products, local_training(): lax.dot_general(tok_rows, residual, (((0,), (0,)), ((), ())), preferred_e...  16.3 us
    dot_general x4, matrix products, local_training(): jnp.dot(tok_rows, weight_bf, preferred_element_type=jnp.float32)  10.8 us
  transfers between devices with their start and end apart: 5, of which 5 were waited for; matrix products, arithmetic and copies ran while one was open for 8% of the time, Pallas kernels for 0%

commit v1 on v0

v1 whole, which is shorter than its diff:
```python
import functools

import jax
import jax.numpy as jnp
from jax import lax
from jax.experimental import pallas as pl
from jax.experimental.pallas import tpu as pltpu
from jax.sharding import PartitionSpec as P

learn_rate = 0.001
beta_one = 0.9
beta_two = 0.95
adam_eps = 1e-08
weight_decay = 0.1
norm_eps = 1e-06

LANES = 128
CORES = 2
YS = 2
PHASES = 7


def flip(index, mask):
    bit = 1
    while bit <= mask:
        if mask & bit:
            index = index + bit - 2 * bit * ((index // bit) % 2)
        bit *= 2
    return index


def train_kernel(
    zs,
    merge,
    weight,
    moment_one_in,
    moment_two_in,
    ids,
    shared_inputs,
    private_inputs,
    shared_targets,
    private_targets,
    out,
    tok,
    tok_t,
    goal,
    moment_one,
    moment_two,
    total,
    weight_b,
    away,
    acc,
    core_in,
    quarter,
    y_in,
    z_in,
    error,
    rep_in,
    dots,
    dots_in,
    send_core,
    recv_core,
    send_y,
    recv_y,
    send_z,
    recv_z,
    send_ez,
    recv_ez,
    send_ey,
    recv_ey,
    send_ec,
    recv_ec,
    send_rep,
    recv_rep,
    send_dot,
    recv_dot,
):
    steps, tokens, depth = tok.shape
    chunks = total.shape[0]
    half = tokens // CORES
    fourth = half // YS
    block = fourth // zs
    out_rows = out.shape[0]
    pool = shared_inputs.shape[0]
    priv = private_inputs.shape[0]

    rep = lax.axis_index("rep")
    row = lax.axis_index("row")
    core = row % CORES
    y = (row // CORES) % YS
    z = row // (CORES * YS)
    other_rep = 1 - rep

    core_dev = (rep, row + 1 - 2 * core)
    y_dev = (rep, row + CORES - 2 * CORES * y)
    z_peer = [flip(z, mask) for mask in range(1, zs)]
    z_dev = [(rep, row + (peer - z) * (CORES * YS)) for peer in z_peer]
    rep_dev = (other_rep, row)

    def remote(src, dst, send_sem, recv_sem, device):
        return pltpu.make_async_remote_copy(
            src_ref=src,
            dst_ref=dst,
            send_sem=send_sem,
            recv_sem=recv_sem,
            device_id=device,
            device_id_type=pl.DeviceIdType.MESH,
        )

    barrier = pltpu.get_barrier_semaphore()
    peers = [core_dev, y_dev] + z_dev + ([rep_dev] if merge else [])
    for device in peers:
        pl.semaphore_signal(
            barrier, inc=1, device_id=device, device_id_type=pl.DeviceIdType.MESH
        )

    def cols(c):
        return slice(c * LANES, (c + 1) * LANES)

    def one_hot(start, size, s, first, count):
        chosen = ids[s, pl.ds(start, size), :]
        spots = lax.broadcasted_iota(jnp.int32, (size, count), 1) + first
        return jnp.where(chosen == spots, 1.0, 0.0).astype(jnp.bfloat16)

    def pick(start, size, s, shared, private):
        return jnp.dot(
            one_hot(start, size, s, 0, pool), shared[...], preferred_element_type=jnp.float32
        ) + jnp.dot(
            one_hot(start, size, s, pool, priv), private[...], preferred_element_type=jnp.float32
        )

    piece = 256 if tokens % 256 == 0 else tokens
    pieces = tokens // piece

    def gather_piece(p, s):
        found = pick(p * piece, piece, s, shared_inputs, private_inputs)
        tok[s, pl.ds(p * piece, piece), :] = found.astype(jnp.bfloat16)
        tok_t[s, :, pl.ds(p * piece, piece)] = found.T.astype(jnp.bfloat16)

    my_row = core * half + y * fourth + z * block

    def gather_goal(s):
        goal[s] = pick(my_row, block, s, shared_targets, private_targets)

    for p in range(pieces):
        gather_piece(p, 0)
    gather_goal(0)
    tile = 128 if depth % 128 == 0 else depth
    for c in range(chunks):
        weight_b[c] = weight[:, cols(c)]
        moment_one[c] = moment_one_in[:, cols(c)].astype(jnp.float32)
        moment_two[c] = moment_two_in[:, cols(c)].astype(jnp.float32)
        total[c] = jnp.zeros((depth, LANES), jnp.float32)
    pl.semaphore_wait(barrier, len(peers))

    def copy_core(c):
        return remote(away.at[c], core_in.at[c], send_core.at[c], recv_core.at[c], core_dev)

    def copy_y(c):
        return remote(
            acc.at[c, pl.ds((1 - y) * fourth, fourth)], y_in.at[c], send_y.at[c], recv_y.at[c], y_dev
        )

    def copy_z(c, d):
        return remote(
            quarter.at[c, pl.ds(z_peer[d] * block, block)],
            z_in.at[c, d],
            send_z.at[c, d],
            recv_z.at[c, d],
            z_dev[d],
        )

    def rows_of(start, size, c):
        return error.at[c, pl.ds(start, size)]

    def spread(c, start, size, send_sem, recv_sem, device):
        return remote(rows_of(start, size, c), rows_of(start, size, c), send_sem, recv_sem, device)

    def send_err_z(c, d):
        return spread(c, my_row, block, send_ez.at[c, d], recv_ez.at[c, d], z_dev[d])

    def land_err_z(c, d):
        start = core * half + y * fourth + z_peer[d] * block
        return spread(c, start, block, send_ez.at[c, d], recv_ez.at[c, d], z_dev[d])

    def send_err_y(c):
        return spread(c, core * half + y * fourth, fourth, send_ey.at[c], recv_ey.at[c], y_dev)

    def land_err_y(c):
        return spread(c, core * half + (1 - y) * fourth, fourth, send_ey.at[c], recv_ey.at[c], y_dev)

    def send_err_core(c):
        return spread(c, core * half, half, send_ec.at[c], recv_ec.at[c], core_dev)

    def land_err_core(c):
        return spread(c, (1 - core) * half, half, send_ec.at[c], recv_ec.at[c], core_dev)

    def copy_rep(c):
        return remote(
            total.at[c, pl.ds(other_rep * out_rows, out_rows)],
            rep_in.at[c],
            send_rep.at[c],
            recv_rep.at[c],
            rep_dev,
        )

    def phase_0(c, s):
        away[c] = jnp.dot(
            tok[s, pl.ds((1 - core) * half, half), :], weight_b[c], preferred_element_type=jnp.float32
        )
        copy_core(c).start()
        acc[c] = jnp.dot(
            tok[s, pl.ds(core * half, half), :], weight_b[c], preferred_element_type=jnp.float32
        )

    def phase_1(c, s):
        copy_core(c).wait()
        theirs = pl.ds((1 - y) * fourth, fourth)
        acc[c, theirs, :] = acc[c, theirs, :] + core_in[c, theirs, :]
        copy_y(c).start()
        mine = pl.ds(y * fourth, fourth)
        quarter[c] = acc[c, mine, :] + core_in[c, mine, :]

    def phase_2(c, s):
        copy_y(c).wait()
        quarter[c] = quarter[c] + y_in[c]
        for d in range(zs - 1):
            copy_z(c, d).start()

    def phase_3(c, s):
        value = quarter[c, pl.ds(z * block, block), :]
        for d in range(zs - 1):
            copy_z(c, d).wait()
            value = value + z_in[c, d]
        residual = (value - goal[s, :, cols(c)]).astype(jnp.bfloat16)
        error[c, pl.ds(my_row, block), :] = residual.astype(jnp.float32)
        for d in range(zs - 1):
            send_err_z(c, d).start()

    def phase_4(c, s):
        for d in range(zs - 1):
            land_err_z(c, d).wait_recv()
        send_err_y(c).start()

    def phase_5(c, s):
        land_err_y(c).wait_recv()
        send_err_core(c).start()

    def phase_6(c, s):
        land_err_core(c).wait_recv()
        residual = error[c].astype(jnp.bfloat16)
        for t in range(depth // tile):
            at = slice(t * tile, (t + 1) * tile)
            gradient = jnp.dot(
                tok_t[s, at, :], residual, preferred_element_type=jnp.float32
            ) / tokens
            start = weight[at, cols(c)].astype(jnp.float32)
            so_far = total[c, at, :]
            m = beta_one * moment_one[c, at, :] + (1.0 - beta_one) * gradient
            v = beta_two * moment_two[c, at, :] + (1.0 - beta_two) * gradient * gradient
            moment_one[c, at, :] = m
            moment_two[c, at, :] = v
            weight_now = start - learn_rate * so_far
            so_far = so_far + (m / (jnp.sqrt(v) + adam_eps) + weight_decay * weight_now)
            total[c, at, :] = so_far
            weight_b[c, at, :] = (start - learn_rate * so_far).astype(jnp.bfloat16)
        for d in range(zs - 1):
            send_err_z(c, d).wait_send()
        send_err_y(c).wait_send()
        send_err_core(c).wait_send()

        if merge:

            @pl.when(s == steps - 1)
            def _():
                copy_rep(c).start()

    phases = (phase_0, phase_1, phase_2, phase_3, phase_4, phase_5, phase_6)
    gap = PHASES // chunks if chunks <= PHASES else 1

    def one_step(s, carry):
        for slot in range(PHASES):
            for c in range(chunks):
                late = slot - gap * c
                back = -(late // PHASES)
                phase = phases[late % PHASES]

                @pl.when(jnp.logical_and(s - back >= 0, s - back < steps))
                def _(c=c, back=back, phase=phase):
                    phase(c, s - back)

            for p in range(pieces):
                if slot == min(1 + p, PHASES - 1):

                    @pl.when(s + 1 < steps)
                    def _(p=p):
                        gather_piece(p, s + 1)

            if slot == PHASES - 2:

                @pl.when(s + 1 < steps)
                def _():
                    gather_goal(s + 1)

        return carry

    extra = -(-(gap * (chunks - 1)) // PHASES)
    lax.fori_loop(0, steps + extra, one_step, 0)

    if not merge:
        for c in range(chunks):
            out[:, cols(c)] = total[c]
        return

    zero = jnp.zeros((8, LANES), jnp.float32)
    cross, own_norm, other_norm = zero, zero, zero

    def fold(values):
        return jnp.sum(values.reshape(out_rows // 8, 8, LANES), axis=0)

    mine = pl.ds(rep * out_rows, out_rows)
    for c in range(chunks):
        copy_rep(c).wait()
        own, far = total[c, mine, :], rep_in[c]
        cross = cross + fold(own * far)
        own_norm = own_norm + fold(own * own)
        other_norm = other_norm + fold(far * far)
    swap = jnp.full((8, LANES), rep, jnp.int32) == 1
    sums = [
        cross,
        jnp.where(swap, other_norm, own_norm),
        jnp.where(swap, own_norm, other_norm),
    ]
    stages = [[rep_dev], [core_dev], [y_dev], z_dev]
    slot = 0
    for number, devices in enumerate(stages):
        for k in range(3):
            dots[number, k] = sums[k]
        copies = []
        for device in devices:
            copies.append(
                remote(
                    dots.at[number],
                    dots_in.at[slot],
                    send_dot.at[slot],
                    recv_dot.at[slot],
                    device,
                )
            )
            slot += 1
        for copy in copies:
            copy.start()
        for place, copy in enumerate(copies):
            copy.wait()
            for k in range(3):
                sums[k] = sums[k] + dots_in[slot - len(copies) + place, k]
    cross, lower, upper = [jnp.sum(s, axis=(0, 1), keepdims=True) for s in sums]
    lower_coef = 1.0 - cross / (2.0 * (lower + norm_eps))
    upper_coef = 1.0 - cross / (2.0 * (upper + norm_eps))
    first = jnp.full((1, 1), rep, jnp.int32) == 0
    own_coef = jnp.where(first, lower_coef, upper_coef)
    far_coef = jnp.where(first, upper_coef, lower_coef)
    for c in range(chunks):
        out[:, cols(c)] = own_coef * total[c, mine, :] + far_coef * rep_in[c]


def from_partner(block, axis, bit):
    count = lax.axis_size(axis)
    route = []
    for low in range(count):
        high = low | 1 << bit
        if high != low and high < count:
            route += [(low, high), (high, low)]
    return lax.ppermute(block, axis, route)


def merge_tree(current):
    replica_count = lax.axis_size("rep")
    level_count = replica_count.bit_length() - 1
    replica = lax.axis_index("rep")
    block_rows = current.shape[0] // replica_count
    for tree_level in range(level_count):
        own_bit = replica // 2**tree_level % 2
        received = from_partner(current, "rep", tree_level)
        lower_vec = jnp.where(own_bit == 0, current, received)
        upper_vec = jnp.where(own_bit == 0, received, current)
        cross_dot, lower_norm, upper_norm = lax.psum(
            (
                jnp.sum(lower_vec * upper_vec),
                jnp.sum(lower_vec * lower_vec),
                jnp.sum(upper_vec * upper_vec),
            ),
            "row",
        )
        lower_coef = 1.0 - cross_dot / (2.0 * (lower_norm + norm_eps))
        upper_coef = 1.0 - cross_dot / (2.0 * (upper_norm + norm_eps))
        current = lower_coef * lower_vec + upper_coef * upper_vec
    return lax.dynamic_slice_in_dim(current, replica * block_rows, block_rows, 0)


def solution(mesh):
    rows = mesh.shape["row"]
    zs = rows // (CORES * YS)
    merge = mesh.shape["rep"] == 2

    def on_device(
        weight,
        first_moment,
        second_moment,
        token_ids,
        shared_inputs,
        private_inputs,
        shared_targets,
        private_targets,
    ):
        depth, columns = weight.shape
        steps, tokens = token_ids.shape[1:]
        chunks = columns // LANES
        half = tokens // CORES
        fourth = half // YS
        block = fourth // zs
        out_rows = depth // 2 if merge else depth
        links = zs - 1 + 3
        dma = pltpu.SemaphoreType.DMA
        f32 = jnp.float32
        pair = [dma((chunks,)), dma((chunks,))]
        pair_z = [dma((chunks, zs - 1)), dma((chunks, zs - 1))]
        result = pl.pallas_call(
            functools.partial(train_kernel, zs, merge),
            out_shape=jax.ShapeDtypeStruct((out_rows, columns), f32),
            in_specs=[pl.BlockSpec(memory_space=pltpu.VMEM)] * 8,
            out_specs=pl.BlockSpec(memory_space=pltpu.VMEM),
            scratch_shapes=[
                pltpu.VMEM((steps, tokens, depth), jnp.bfloat16),
                pltpu.VMEM((steps, depth, tokens), jnp.bfloat16),
                pltpu.VMEM((steps, block, columns), f32),
                pltpu.VMEM((chunks, depth, LANES), f32),
                pltpu.VMEM((chunks, depth, LANES), f32),
                pltpu.VMEM((chunks, depth, LANES), f32),
                pltpu.VMEM((chunks, depth, LANES), jnp.bfloat16),
                pltpu.VMEM((chunks, half, LANES), f32),
                pltpu.VMEM((chunks, half, LANES), f32),
                pltpu.VMEM((chunks, half, LANES), f32),
                pltpu.VMEM((chunks, fourth, LANES), f32),
                pltpu.VMEM((chunks, fourth, LANES), f32),
                pltpu.VMEM((chunks, zs - 1, block, LANES), f32),
                pltpu.VMEM((chunks, tokens, LANES), f32),
                pltpu.VMEM((chunks, out_rows, LANES), f32),
                pltpu.VMEM((4, 3, 8, LANES), f32),
                pltpu.VMEM((links, 3, 8, LANES), f32),
            ]
            + pair
            + pair
            + pair_z
            + pair_z
            + pair
            + pair
            + pair
            + [dma((links,)), dma((links,))],
            compiler_params=pltpu.CompilerParams(
                collective_id=0, has_side_effects=True, vmem_limit_bytes=56 * 1024 * 1024
            ),
        )(
            weight,
            first_moment[0],
            second_moment[0],
            token_ids[0][:, :, None],
            shared_inputs,
            private_inputs[0],
            shared_targets,
            private_targets[0],
        )
        return result if merge else merge_tree(result)

    placed = (
        P("row", None),
        P("rep", "row", None),
        P("rep", "row", None),
        P("rep", None, None),
        P(None, "row"),
        P("rep", None, "row"),
        P(),
        P("rep", None, None),
    )
    return jax.shard_map(
        on_device, mesh=mesh, in_specs=placed, out_specs=P(("row", "rep"), None), check_vma=False
    )
```

time: 486 us -> 164 us (0.34)
  waiting for transfers between devices: 360 us -> 0 us
  Pallas kernels: 0 us -> 160 us
  local copies, waits for them, and re-layouts: 46.1 us -> 4.48 us
  blocking collectives: 30.2 us -> 0 us
  matrix products: 27.1 us -> 0 us
  between operations: 15.8 us -> 0.01 us
    psum x4 -> x0, waiting for transfers between devices: 343 us -> none  [local_training(): output = lax.psum(partial_value, 'row')]
    pallas_call x0 -> x1, Pallas kernels: none -> 160 us  [on_device(): pl.pallas_call(functools.partial(train_kernel, zs, merge), out_shape=jax....]
    gather x8 -> x0, local copies, waits for them, and re-layouts: 42.1 us -> none  [the longest x4 23 us: local_training(): tok_rows = jnp.take(input_table, chosen, axis=0)]
    psum x1 -> x0, blocking collectives: 30.2 us -> none  [on_device(): lax.psum((local_dots[0], local_dots[1], local_dots[2]), 'row')]
    dot_general x8 -> x0, matrix products: 27.1 us -> none  [the longest x4 16.3 us: local_training(): lax.dot_general(tok_rows, residual, (((0,), (0,)), ((), ())), preferred_e...]
    ppermute x1 -> x0, waiting for transfers between devices: 16.8 us -> none  [from_partner(): return lax.ppermute(block, axis, route)]
  transfers between devices with their start and end apart: 5 -> 0, of which waited for: 5 -> 0; matrix products, arithmetic and copies ran while one was open for 8% -> 0% of each run, Pallas kernels for 0% -> 0%
where the time goes in v1:
time: 164 us
  Pallas kernels  160 us (98%)
  local copies, waits for them, and re-layouts  4.48 us (3%)
    pallas_call x1, Pallas kernels, on_device(): pl.pallas_call(functools.partial(train_kernel, zs, merge), out_shape=jax....  160 us

profile of v1, /device:TPU:0, one launch (start us, length us, event | category | flops | bytes accessed | tf_op | source)
XLA Modules:
  0.0 164.1 jit_solution(8084187018226640939)
XLA Ops:
  0.0 2.7 %copy.9.ids = s32[4,1024,1]{2,1,0:T(8,128)} copy(s32[4,1024,1]{1,0,2:T(4,128)} %bitcast.9) | data formatting | bytes 32768 | tf_op jit(solution)/shard_map/broadcast_in_dim;squeeze | solution.py:467
  2.7 159.6 %shard_map.82 = f32[256,384]{1,0:T(8,128)} custom-call(bf16[512,384]{1,0:T(8,128)(2,1)} %weight.1, bf16[512,384]{1,0:T(8,128)(2,1)} %bitcast.6, bf16[512,384]{1,0:T(8,128)(2,1)} %bitcast.7, s32[4,1024,1]{2,1,0:T(8,128)} %copy.9.ids, bf16[1024,512]{1,0:T(8,128)(2,1)} %shared_inputs.1, bf16[512,512]{1,0:T(8,128)(2,1)} %bitcast.5, ...), custom_call_target="tpu_custom_call" | custom-call | tf_op jit(solution)/shard_map/pallas_call | solution.py:428
  162.3 1.8 %copy.11 = f32[256,384]{1,0:T(8,128)} copy(f32[256,384]{1,0:T(8,128)} %shard_map.82) | data formatting | bytes 786432

commit v2 on v1

--- a/solution.py
+++ b/solution.py
@@ -153,12 +153,25 @@
         total[c] = jnp.zeros((depth, LANES), jnp.float32)
     pl.semaphore_wait(barrier, len(peers))
 
-    def copy_core(c):
-        return remote(away.at[c], core_in.at[c], send_core.at[c], recv_core.at[c], core_dev)
-
-    def copy_y(c):
+    z_order = z_peer + [z]
+
+    def copy_core(c, k):
+        if k < zs:
+            at = pl.ds((1 - y) * fourth + z_order[k] * block, block)
+        else:
+            at = pl.ds(y * fourth, fourth)
         return remote(
-            acc.at[c, pl.ds((1 - y) * fourth, fourth)], y_in.at[c], send_y.at[c], recv_y.at[c], y_dev
+            away.at[c, at], core_in.at[c, at], send_core.at[c, k], recv_core.at[c, k], core_dev
+        )
+
+    def copy_y(c, k):
+        at = pl.ds((1 - y) * fourth + z_order[k] * block, block)
+        return remote(
+            acc.at[c, at],
+            y_in.at[c, pl.ds(z_order[k] * block, block)],
+            send_y.at[c, k],
+            recv_y.at[c, k],
+            y_dev,
         )
 
     def copy_z(c, d):
@@ -170,30 +183,37 @@
             z_dev[d],
         )
 
-    def rows_of(start, size, c):
-        return error.at[c, pl.ds(start, size)]
-
-    def spread(c, start, size, send_sem, recv_sem, device):
-        return remote(rows_of(start, size, c), rows_of(start, size, c), send_sem, recv_sem, device)
+    def spread(c, start, send_sem, recv_sem, device):
+        at = error.at[c, pl.ds(start, block)]
+        return remote(at, at, send_sem, recv_sem, device)
+
+    def place_of(core_at, y_at, z_at):
+        return core_at * half + y_at * fourth + z_at * block
 
     def send_err_z(c, d):
-        return spread(c, my_row, block, send_ez.at[c, d], recv_ez.at[c, d], z_dev[d])
+        return spread(c, my_row, send_ez.at[c, d], recv_ez.at[c, d], z_dev[d])
 
     def land_err_z(c, d):
-        start = core * half + y * fourth + z_peer[d] * block
-        return spread(c, start, block, send_ez.at[c, d], recv_ez.at[c, d], z_dev[d])
-
-    def send_err_y(c):
-        return spread(c, core * half + y * fourth, fourth, send_ey.at[c], recv_ey.at[c], y_dev)
-
-    def land_err_y(c):
-        return spread(c, core * half + (1 - y) * fourth, fourth, send_ey.at[c], recv_ey.at[c], y_dev)
-
-    def send_err_core(c):
-        return spread(c, core * half, half, send_ec.at[c], recv_ec.at[c], core_dev)
-
-    def land_err_core(c):
-        return spread(c, (1 - core) * half, half, send_ec.at[c], recv_ec.at[c], core_dev)
+        start = place_of(core, y, z_peer[d])
+        return spread(c, start, send_ez.at[c, d], recv_ez.at[c, d], z_dev[d])
+
+    def send_err_y(c, k):
+        start = place_of(core, y, z_order[k])
+        return spread(c, start, send_ey.at[c, k], recv_ey.at[c, k], y_dev)
+
+    def land_err_y(c, k):
+        start = place_of(core, 1 - y, z_order[k])
+        return spread(c, start, send_ey.at[c, k], recv_ey.at[c, k], y_dev)
+
+    def send_err_core(c, side, k):
+        n = side * zs + k
+        start = place_of(core, y + side * (1 - 2 * y), z_order[k])
+        return spread(c, start, send_ec.at[c, n], recv_ec.at[c, n], core_dev)
+
+    def land_err_core(c, side, k):
+        n = side * zs + k
+        start = place_of(1 - core, y + side * (1 - 2 * y), z_order[k])
+        return spread(c, start, send_ec.at[c, n], recv_ec.at[c, n], core_dev)
 
     def copy_rep(c):
         return remote(
@@ -204,28 +224,37 @@
             rep_dev,
         )
 
+    def forward(c, s, core_at, y_at):
+        start = core_at * half + y_at * fourth
+        return jnp.dot(
+            tok[s, pl.ds(start, fourth), :], weight_b[c], preferred_element_type=jnp.float32
+        )
+
     def phase_0(c, s):
-        away[c] = jnp.dot(
-            tok[s, pl.ds((1 - core) * half, half), :], weight_b[c], preferred_element_type=jnp.float32
-        )
-        copy_core(c).start()
-        acc[c] = jnp.dot(
-            tok[s, pl.ds(core * half, half), :], weight_b[c], preferred_element_type=jnp.float32
-        )
+        away[c, pl.ds((1 - y) * fourth, fourth), :] = forward(c, s, 1 - core, 1 - y)
+        for k in range(zs):
+            copy_core(c, k).start()
+        away[c, pl.ds(y * fourth, fourth), :] = forward(c, s, 1 - core, y)
+        copy_core(c, zs).start()
+        acc[c, pl.ds((1 - y) * fourth, fourth), :] = forward(c, s, core, 1 - y)
+        acc[c, pl.ds(y * fourth, fourth), :] = forward(c, s, core, y)
 
     def phase_1(c, s):
-        copy_core(c).wait()
-        theirs = pl.ds((1 - y) * fourth, fourth)
-        acc[c, theirs, :] = acc[c, theirs, :] + core_in[c, theirs, :]
-        copy_y(c).start()
-        mine = pl.ds(y * fourth, fourth)
-        quarter[c] = acc[c, mine, :] + core_in[c, mine, :]
+        for k in range(zs):
+            copy_core(c, k).wait()
+            at = pl.ds((1 - y) * fourth + z_order[k] * block, block)
+            acc[c, at, :] = acc[c, at, :] + core_in[c, at, :]
+            copy_y(c, k).start()
 
     def phase_2(c, s):
-        copy_y(c).wait()
-        quarter[c] = quarter[c] + y_in[c]
-        for d in range(zs - 1):
-            copy_z(c, d).start()
+        copy_core(c, zs).wait()
+        for k in range(zs):
+            copy_y(c, k).wait()
+            at = pl.ds(z_order[k] * block, block)
+            own = pl.ds(y * fourth + z_order[k] * block, block)
+            quarter[c, at, :] = acc[c, own, :] + core_in[c, own, :] + y_in[c, at, :]
+            if k < zs - 1:
+                copy_z(c, k).start()
 
     def phase_3(c, s):
         value = quarter[c, pl.ds(z * block, block), :]
@@ -236,18 +265,26 @@
         error[c, pl.ds(my_row, block), :] = residual.astype(jnp.float32)
         for d in range(zs - 1):
             send_err_z(c, d).start()
+        send_err_y(c, zs - 1).start()
+        send_err_core(c, 0, zs - 1).start()
 
     def phase_4(c, s):
         for d in range(zs - 1):
             land_err_z(c, d).wait_recv()
-        send_err_y(c).start()
+            send_err_y(c, d).start()
+            send_err_core(c, 0, d).start()
+
+    early_first = [zs - 1] + list(range(zs - 1))
 
     def phase_5(c, s):
-        land_err_y(c).wait_recv()
-        send_err_core(c).start()
+        for k in early_first:
+            land_err_y(c, k).wait_recv()
+            send_err_core(c, 1, k).start()
 
     def phase_6(c, s):
-        land_err_core(c).wait_recv()
+        for side in range(YS):
+            for k in early_first:
+                land_err_core(c, side, k).wait_recv()
         residual = error[c].astype(jnp.bfloat16)
         for t in range(depth // tile):
             at = slice(t * tile, (t + 1) * tile)
@@ -266,8 +303,10 @@
             weight_b[c, at, :] = (start - learn_rate * so_far).astype(jnp.bfloat16)
         for d in range(zs - 1):
             send_err_z(c, d).wait_send()
-        send_err_y(c).wait_send()
-        send_err_core(c).wait_send()
+        for k in range(zs):
+            send_err_y(c, k).wait_send()
+            for side in range(YS):
+                send_err_core(c, side, k).wait_send()
 
         if merge:
 
@@ -423,8 +462,10 @@
         links = zs - 1 + 3
         dma = pltpu.SemaphoreType.DMA
         f32 = jnp.float32
-        pair = [dma((chunks,)), dma((chunks,))]
-        pair_z = [dma((chunks, zs - 1)), dma((chunks, zs - 1))]
+
+        def pair_of(count):
+            return [dma((chunks, count)), dma((chunks, count))]
+
         result = pl.pallas_call(
             functools.partial(train_kernel, zs, merge),
             out_shape=jax.ShapeDtypeStruct((out_rows, columns), f32),
@@ -449,13 +490,13 @@
                 pltpu.VMEM((4, 3, 8, LANES), f32),
                 pltpu.VMEM((links, 3, 8, LANES), f32),
             ]
-            + pair
-            + pair
-            + pair_z
-            + pair_z
-            + pair
-            + pair
-            + pair
+            + pair_of(zs + 1)
+            + pair_of(zs)
+            + pair_of(zs - 1)
+            + pair_of(zs - 1)
+            + pair_of(zs)
+            + pair_of(YS * zs)
+            + [dma((chunks,)), dma((chunks,))]
             + [dma((links,)), dma((links,))],
             compiler_params=pltpu.CompilerParams(
                 collective_id=0, has_side_effects=True, vmem_limit_bytes=56 * 1024 * 1024

time: 164 us -> 156 us (0.951)
  Pallas kernels: 160 us -> 151 us
    pallas_call x1, Pallas kernels: 160 us -> 151 us  [on_device(): pl.pallas_call(functools.partial(train_kernel, zs, merge), out_shape=jax....]
where the time goes in v2:
time: 156 us
  Pallas kernels  151 us (97%)
  local copies, waits for them, and re-layouts  4.48 us (3%)
    pallas_call x1, Pallas kernels, on_device(): pl.pallas_call(functools.partial(train_kernel, zs, merge), out_shape=jax....  151 us

profile of v2, /device:TPU:0, one launch (start us, length us, event | category | flops | bytes accessed | tf_op | source)
XLA Modules:
  0.0 156.0 jit_solution(10558231311714663029)
XLA Ops:
  0.0 2.7 %copy.9.ids = s32[4,1024,1]{2,1,0:T(8,128)} copy(s32[4,1024,1]{1,0,2:T(4,128)} %bitcast.9) | data formatting | bytes 32768 | tf_op jit(solution)/shard_map/broadcast_in_dim;squeeze | solution.py:508
  2.7 151.5 %shard_map.82 = f32[256,384]{1,0:T(8,128)} custom-call(bf16[512,384]{1,0:T(8,128)(2,1)} %weight.1, bf16[512,384]{1,0:T(8,128)(2,1)} %bitcast.6, bf16[512,384]{1,0:T(8,128)(2,1)} %bitcast.7, s32[4,1024,1]{2,1,0:T(8,128)} %copy.9.ids, bf16[1024,512]{1,0:T(8,128)(2,1)} %shared_inputs.1, bf16[512,512]{1,0:T(8,128)(2,1)} %bitcast.5, ...), custom_call_target="tpu_custom_call" | custom-call | tf_op jit(solution)/shard_map/pallas_call | solution.py:469
  154.2 1.8 %copy.11 = f32[256,384]{1,0:T(8,128)} copy(f32[256,384]{1,0:T(8,128)} %shard_map.82) | data formatting | bytes 786432
